TPU v7x, 128 devices: a whole 4x4x4 slice. The times are simulated.
128 devices in a mesh: section: 2 (over z_lo), patch: 4 (over y), shard: 16 (over z_hi, x, core).
Axes of the slice: x: 4, y: 4, z: 4 (z_hi: 2, z_lo: 2; z = z_hi * 2 + z_lo), core: 2. Of those that a mesh axis runs over, the one named last changes fastest.
Arguments:
- hidden: bfloat16 [32, 1024, 2432], P('shard', 'patch'), may hold values from -6 to 6
- text_kv: bfloat16 [2, 32, 154, 2432], P('section', 'shard'), may hold values from -6 to 6, as said below
- stale_kv: bfloat16 [2, 32, 1024, 2432], P('section', 'shard', 'patch'), may hold values from -6 to 6, as said below
- modulation: float32 [2, 32, 3, 2432], P('section', 'shard'), may hold values from -3 to 3
- score_gain: float32 [2, 64], P('section'), may hold values from 1.5 to 4
- qkv_weight: bfloat16 [2, 2432, 3648], P('section', 'shard'), may hold values from -0.125 to 0.125
- out_weight: bfloat16 [2, 1216, 2432], P('section', None, 'shard'), may hold values from -0.15625 to 0.15625
- final_mod: float32 [32, 2, 2432], P('shard'), may hold values from -3 to 3
- final_weight: bfloat16 [2432, 64], replicated, may hold values from -0.125 to 0.125
- latent: float32 [32, 1024, 64], P('shard', ('patch', 'section')), may hold values from -6 to 6
- step_index: int32 [32], P('shard'), may hold values from 0 to 27
Outputs:
- new_kv: bfloat16 [2, 32, 1024, 2432], P('section', 'shard', 'patch')
- latent_next: float32 [32, 1024, 64], P('shard', ('patch', 'section'))
- denoised: float32 [32, 1024, 64], P('shard', ('patch', 'section'))
Inputs may be any that keep to these rules, and one draw needn't show every extreme that they name: `text_kv`: in every row the first 1216 columns are 19 heads of 64 key features, each head with mean square one up to bfloat16 rounding. `stale_kv`: in every row the first 1216 columns are 19 heads of 64 key features, each head with mean square one up to bfloat16 rounding.
All inputs are finite; a program needn't handle non-finite values.
Results may differ from a plain program's by a relative error of at most 0.008.
Values may be sent and summed in bfloat16 or wider, within the bound.
No kernel may reach another device: no remote copies, remote signals or barrier semaphores. Data moves between devices by JAX's collectives and lax.ppermute only.
A program may use at most 192 MiB of HBM per device.

v0:
```python
import math
import jax
import jax.numpy as jnp
from jax import lax
from jax.sharding import PartitionSpec as P

HEAD = 64
NSTEPS = 28
eps_norm = 1e-06
flow_shift = 3.0


def passed_along(value, axis, steps):
    count = lax.axis_size(axis)
    first, last = (max(0, -steps), min(count, count - steps))
    return lax.ppermute(value, axis, [(source, source + steps) for source in range(first, last)])


def spread(array, axis, root):
    mine = lax.axis_index(axis) == root
    return lax.psum(jnp.where(mine, array, jnp.zeros_like(array)), axis)


def sigma_of(step):
    s = 1.0 - step.astype(jnp.float32) / NSTEPS
    return flow_shift * s / (1.0 + (flow_shift - 1.0) * s)


def modulated(xf, shift, scale):
    mean = jnp.mean(xf, -1, keepdims=True)
    cent = xf - mean
    var = jnp.mean(cent * cent, -1, keepdims=True)
    return cent * lax.rsqrt(var + eps_norm) * (1.0 + scale) + shift


def attend_one(query, keys_all, width, heads):
    count = keys_all.shape[0]
    keys = keys_all[:, :width].reshape(count, heads, HEAD)
    values = keys_all[:, width:].reshape(count, heads, HEAD)
    scores = jnp.einsum("qhe,khe->hqk", query, keys, preferred_element_type=jnp.float32)
    expo = jnp.exp(scores)
    total = jnp.sum(expo, -1)
    weights = expo.astype(jnp.bfloat16)
    mixed = jnp.einsum("hqk,khe->qhe", weights, values, preferred_element_type=jnp.float32)
    mixed = mixed / jnp.transpose(total)[:, :, None]
    return mixed.reshape(query.shape[0], width).astype(jnp.bfloat16)


def run_layer(x, stale_all, text_one, mod_one, gain, w_qkv, w_out, patch_index):
    requests, rows = (x.shape[0], x.shape[1])
    width = w_out.shape[0]
    heads = width // HEAD
    xf = x.astype(jnp.float32)
    normed = modulated(xf, mod_one[:, 0:1, :], mod_one[:, 1:2, :]).astype(jnp.bfloat16)
    proj_in = jnp.einsum("rid,dc->ric", normed, w_qkv, preferred_element_type=jnp.float32)
    q = proj_in[..., :width].reshape(requests, rows, heads, HEAD)
    k = proj_in[..., width : 2 * width].reshape(requests, rows, heads, HEAD)
    v = proj_in[..., 2 * width :]
    q_hat = q * lax.rsqrt(jnp.mean(q * q, -1, keepdims=True) + eps_norm)
    k_hat = k * lax.rsqrt(jnp.mean(k * k, -1, keepdims=True) + eps_norm)
    fresh = jnp.concatenate(
        [k_hat.reshape(requests, rows, width).astype(jnp.bfloat16), v.astype(jnp.bfloat16)], -1
    )
    query = (q_hat * gain / math.sqrt(HEAD)).astype(jnp.bfloat16)
    mixed = lax.dynamic_update_slice_in_dim(stale_all, fresh, patch_index * rows, 1)
    keys_all = jnp.concatenate([text_one, mixed], 1)

    def per_request(pair):
        return attend_one(pair[0], pair[1], width, heads)

    attn = lax.map(per_request, (query, keys_all))
    proj = jnp.einsum("riw,wd->rid", attn, w_out, preferred_element_type=jnp.float32)
    x_next = (xf + mod_one[:, 2:3, :] * proj).astype(jnp.bfloat16)
    return (x_next, fresh)


def on_device(
    hidden,
    text_kv,
    stale_kv,
    modulation,
    score_gain,
    qkv_weight,
    out_weight,
    final_mod,
    final_weight,
    latent,
    step_index,
):
    w_qkv, w_out = (
        lax.all_gather(qkv_weight[0], "shard", axis=0, tiled=True),
        lax.all_gather(out_weight[0], "shard", axis=1, tiled=True),
    )
    stale_all = lax.all_gather(stale_kv[0], "patch", axis=1, tiled=True)
    section = lax.axis_index("section")
    patch_index = lax.axis_index("patch")

    def compute(x):
        return run_layer(
            x, stale_all, text_kv[0], modulation[0], score_gain[0], w_qkv, w_out, patch_index
        )

    def passing(x):
        return (x, jnp.zeros(stale_kv.shape[1:], jnp.bfloat16))

    first, fresh_first = lax.cond(section == 0, compute, passing, hidden)
    arrived = passed_along(first, "section", 1)
    last, fresh_last = lax.cond(section == 1, compute, passing, arrived)
    fresh = jnp.where(section == 0, fresh_first, fresh_last)
    final = modulated(last.astype(jnp.float32), final_mod[:, 0:1, :], final_mod[:, 1:2, :]).astype(
        jnp.bfloat16
    )
    velocity = jnp.einsum("rid,dc->ric", final, final_weight, preferred_element_type=jnp.float32)
    half = latent.shape[1]
    shared = spread(velocity.astype(jnp.bfloat16), "section", 1).astype(velocity.dtype)
    velocity_mine = lax.dynamic_slice_in_dim(shared, section * half, half, 1)
    sig = sigma_of(step_index)[:, None, None]
    sig_next = sigma_of(step_index + 1)[:, None, None]
    latent_next = latent + (sig_next - sig) * velocity_mine
    denoised = latent - sig * velocity_mine
    return (fresh[None], latent_next, denoised)


def solution(mesh):
    in_specs = (
        P("shard", "patch", None),
        P("section", "shard", None, None),
        P("section", "shard", "patch", None),
        P("section", "shard", None, None),
        P("section", None),
        P("section", "shard", None),
        P("section", None, "shard"),
        P("shard", None, None),
        P(),
        P("shard", ("patch", "section"), None),
        P("shard"),
    )
    out_specs = (
        P("section", "shard", "patch", None),
        P("shard", ("patch", "section"), None),
        P("shard", ("patch", "section"), None),
    )
    return jax.shard_map(
        on_device, mesh=mesh, in_specs=in_specs, out_specs=out_specs, check_vma=False
    )
```

profile of v0, /device:TPU:1, one launch (start us, length us, event | category | flops | bytes accessed | tf_op | source)
XLA Modules:
  0.0 642.9 jit_solution(3232019068005679391)
XLA Ops:
  8.0 4.5 copy.28
  13.3 64.7 %all-gather.11.cloned.1.call-done = bf16[1,1216,2432]{1,2,0:T(8,128)(2,1)} async-done(((bf16[1,1216,152]{1,2,0:T(8,128)(2,1)}), bf16[1,1216,2432]{1,2,0:T(8,128)(2,1)}) %all-gather.11.cloned.1.call-update) | async-done | bytes 5914640 | tf_op jit(solution)/shard_map/all_gather | solution.py:92
  78.0 100.0 %all-gather.9.cloned.1.call-done = bf16[1,2,1024,2432]{2,3,1,0:T(8,128)(2,1)} async-done(((bf16[1,2,256,2432]{2,3,1,0:T(8,128)(2,1)}), bf16[1,2,1024,2432]{2,3,1,0:T(8,128)(2,1)}) %all-gather.9.cloned.1.call-update) | async-done | bytes 9961488 | tf_op jit(solution)/shard_map/all_gather | solution.py:94
  177.9 120.4 %all-gather.7.cloned.1.call-done = bf16[1,2432,3648]{2,1,0:T(8,128)(2,1)} async-done(((bf16[1,152,3648]{2,1,0:T(8,128)(2,1)}), bf16[1,2432,3648]{2,1,0:T(8,128)(2,1)}) %all-gather.7.cloned.1.call-update) | async-done | bytes 17743888 | tf_op jit(solution)/shard_map/all_gather | solution.py:91
  298.4 129.6 %conditional.2 = (bf16[2,256,2432]{2,1,0:T(8,128)(2,1)S(1)}, bf16[2,256,2432]{2,1,0:T(8,128)(2,1)}) conditional(s32[]{:T(128)} %convert_element_type.88, bf16[2,256,2432]{2,1,0:T(8,128)(2,1)S(1)} %copy-done.2, (bf16[2,256,2432]{2,1,0:T(8,128)(2,1)S(1)}, f32[1,2,3,2432]{3,1,2,0:T(2,128)S(1)}, bf16[2432,3648]{1,0:T(8,128)(2,1)}, f32[1,64]{1,0:T(1,128)S(1)}, ...), branch_computations={%region_0.0_spmd, %region_1.9_spmd} | conditional | flops 13646128128 | bytes 220811024 | solution.py:106
  300.2 16.5 %fusion.6 = f32[2,256,3648]{1,2,0:T(8,128)} fusion(bf16[2432,3648]{1,0:T(8,128)(2,1)} %get-tuple-element.139, bf16[2,256,2432]{2,1,0:T(8,128)(2,1)S(1)} %get-tuple-element.71, f32[2,2432]{1,0:T(2,128)S(1)} %get-tuple-element.182, f32[2,2432]{1,0:T(2,128)S(1)} %get-tuple-element.183, f32[2,256]{1,0:T(2,128)S(1)} %add_rsqrt_fusion.2, ...), kind=kOutput, calls=%fused_computation.11 | convolution fusion | flops 9092333568 | bytes 27748352 | tf_op jit(solution)/shard_map/cond/branch_1_fun/rid,dc->ric/dot_general | solution.py:55
  316.7 3.3 slice_multiply_fusion
  320.1 2.0 reduce_sum.99
  322.1 4.7 fusion.76
  326.7 2.9 slice.91
  329.6 8.8 %copy.62 = bf16[2,1024,2432]{1,2,0:T(8,128)(2,1)} copy(bf16[2,1024,2432]{1,2,0:T(8,128)(2,1)} %get-tuple-element.74) | data formatting | bytes 19922944 | tf_op jit(solution)/shard_map/cond
  338.4 4.3 pad_maximum_fusion.1
  342.7 5.8 copy.30
  348.5 13.1 %pad_maximum_fusion = bf16[2,1178,2432]{1,2,0:T(8,128)(2,1)} fusion(bf16[2,1024,2432]{1,2,0:T(8,128)(2,1)} %get-tuple-element.180, bf16[2,154,2432]{1,2,0:T(8,128)(2,1)} %bitcast.147), kind=kLoop, calls=%fused_computation.13 | loop fusion | flops 22919168 | bytes 22919168 | tf_op jit(solution)/shard_map/cond/branch_1_fun/concatenate | solution.py:66
  361.9 1.5 multiply_convert_fusion
  363.5 52.4 %while.18 = (s32[]{:T(128)}, bf16[2,256,1216]{1,2,0:T(8,128)(2,1)}, bf16[2,1178,2432]{1,2,0:T(8,128)(2,1)}, bf16[2,256,19,64]{1,3,2,0:T(8,128)(2,1)}, s32[]{:T(128)}) while((s32[]{:T(128)}, bf16[2,256,1216]{1,2,0:T(8,128)(2,1)}, bf16[2,1178,2432]{1,2,0:T(8,128)(2,1)}, bf16[2,256,19,64]{1,3,2,0:T(8,128)(2,1)}, s32[]{:T(128)}) %tuple.88), condition=%wide.region_8.8_spmd, body=%wide.region_6.7_spmd.sunk | while | flops 1478904064 | bytes 82245984 | solution.py:71
  364.0 3.2 dynamic-slice_bitcast_fusion.5
  368.4 9.7 %exponential_reduce_fusion.5 = (f32[19,256]{1,0:T(8,128)S(1)}, f32[19,256,1178]{1,2,0:T(8,128)}) fusion(bf16[1178,19,64]{0,2,1:T(8,128)(2,1)S(1)} %bitcast.134, bf16[2,256,19,64]{1,3,2,0:T(8,128)(2,1)S(1)} %copy-done.5, s32[]{:T(128)} %get-tuple-element.287), kind=kOutput, calls=%fused_computation.clone.1 | convolution fusion | flops 739138304 | bytes 26674180 | tf_op jit(solution)/shard_map/cond/branch_1_fun/while/body/eval_jaxpr/qhe,khe->hqk/dot_general | solution.py:40
  378.1 10.9 %divide_convert_fusion.5 = bf16[256,19,64]{0,2,1:T(8,128)(2,1)S(1)} fusion(bf16[1178,19,64]{0,2,1:T(8,128)(2,1)S(1)} %bitcast.136, f32[19,256,1178]{1,2,0:T(8,128)} %get-tuple-element.265, f32[256,19]{0,1:T(8,128)S(1)} %bitcast.150), kind=kOutput, calls=%fused_computation.5.clone.1 | convolution fusion | flops 739765760 | bytes 26426112 | tf_op jit(solution)/shard_map/cond/branch_1_fun/while/body/eval_jaxpr/hqk,khe->qhe/dot_general | solution.py:44
  389.9 3.2 dynamic-slice_bitcast_fusion.5
  394.4 9.7 %exponential_reduce_fusion.5 = (f32[19,256]{1,0:T(8,128)S(1)}, f32[19,256,1178]{1,2,0:T(8,128)}) fusion(bf16[1178,19,64]{0,2,1:T(8,128)(2,1)S(1)} %bitcast.134, bf16[2,256,19,64]{1,3,2,0:T(8,128)(2,1)S(1)} %copy-done.5, s32[]{:T(128)} %get-tuple-element.287), kind=kOutput, calls=%fused_computation.clone.1 | convolution fusion | flops 739138304 | bytes 26674180 | tf_op jit(solution)/shard_map/cond/branch_1_fun/while/body/eval_jaxpr/qhe,khe->hqk/dot_general | solution.py:40
  404.1 10.9 %divide_convert_fusion.5 = bf16[256,19,64]{0,2,1:T(8,128)(2,1)S(1)} fusion(bf16[1178,19,64]{0,2,1:T(8,128)(2,1)S(1)} %bitcast.136, f32[19,256,1178]{1,2,0:T(8,128)} %get-tuple-element.265, f32[256,19]{0,1:T(8,128)S(1)} %bitcast.150), kind=kOutput, calls=%fused_computation.5.clone.1 | convolution fusion | flops 739765760 | bytes 26426112 | tf_op jit(solution)/shard_map/cond/branch_1_fun/while/body/eval_jaxpr/hqk,khe->qhe/dot_general | solution.py:44
  415.9 7.6 %fusion.19 = bf16[2,256,2432]{2,1,0:T(8,128)(2,1)S(1)} fusion(bf16[2,256,2432]{2,1,0:T(8,128)(2,1)S(1)} %get-tuple-element.71, bf16[2,256,1216]{1,2,0:T(8,128)(2,1)} %get-tuple-element.78, bf16[1216,2432]{0,1:T(8,128)(2,1)} %get-tuple-element.144, f32[2,2432]{1,0:T(2,128)S(1)} %copy-done.10), kind=kOutput, calls=%fused_computation.26 | convolution fusion | flops 3033268224 | bytes 12160000 | tf_op jit(solution)/shard_map/cond/branch_1_fun/riw,wd->rid/dot_general | solution.py:72
  423.5 4.3 copy.46
  428.0 1.5 copy-done.1
  432.2 52.4 %collective-permute-done = bf16[2,256,2432]{2,1,0:T(8,128)(2,1)S(1)} collective-permute-done((bf16[2,256,2432]{2,1,0:T(8,128)(2,1)}, bf16[2,256,2432]{2,1,0:T(8,128)(2,1)S(1)}, u32[]{:S(2)}, u32[]{:S(2)}) %collective-permute-start) | collective-permute-done | bytes 2490400 | tf_op jit(solution)/shard_map/ppermute | solution.py:16
  484.6 4.3 conditional.3
  484.6 1.6 broadcast.161.clone
  490.2 1.8 fusion.69
  492.0 3.4 select_bitcast_fusion
  495.5 138.9 %all-reduce.2.cloned.1.call-done = bf16[2,256,64]{1,2,0:T(8,128)(2,1)} async-done(((bf16[2,256,64]{1,2,0:T(8,128)(2,1)}), bf16[2,256,64]{1,2,0:T(8,128)(2,1)}) %all-reduce.2.cloned.1.call-update) | async-done | bytes 65552 | tf_op jit(solution)/shard_map/psum | solution.py:21
  634.4 1.5 fusion.73
  (60 shorter events, 12.0 us)
Async XLA Ops:
  7.2 483.0 %copy-start = (bf16[2432,64]{0,1:T(8,128)(2,1)S(1)}, bf16[2432,64]{0,1:T(8,128)(2,1)}, u32[]{:S(2)}) copy-start(bf16[2432,64]{0,1:T(8,128)(2,1)} %param.27) | copy-start | bytes 933892
  7.2 70.8 %all-gather.11.cloned.1.call-start = ((), (), s32[]{:S(2)}) async-start(), calls=%async_computation.3 | async-start | bytes 6615040 | tf_op jit(solution)/shard_map/all_gather | solution.py:92
  7.9 290.4 %copy-start.2 = (bf16[2,256,2432]{2,1,0:T(8,128)(2,1)S(1)}, bf16[2,256,2432]{2,1,0:T(8,128)(2,1)}, u32[]{:S(2)}) copy-start(bf16[2,256,2432]{2,1,0:T(8,128)(2,1)} %param.19) | copy-start | bytes 7471108
  7.9 290.4 %copy-start.7 = (f32[1,2,3,2432]{3,1,2,0:T(2,128)S(1)}, f32[1,2,3,2432]{3,1,2,0:T(2,128)}, u32[]{:S(2)}) copy-start(f32[1,2,3,2432]{3,1,2,0:T(2,128)} %param.22) | copy-start | bytes 175108
  7.9 290.4 %copy-start.14 = (f32[1,64]{1,0:T(1,128)S(1)}, f32[1,64]{1,0:T(1,128)}, u32[]{:S(2)}) copy-start(f32[1,64]{1,0:T(1,128)} %param.23) | copy-start | bytes 772
  7.9 170.0 %all-gather.9.cloned.1.call-start = ((), (), s32[]{:S(2)}) async-start(), calls=%async_computation.2 | async-start | bytes 12451840 | tf_op jit(solution)/shard_map/all_gather | solution.py:94
  12.5 285.9 %all-gather.7.cloned.1.call-start = ((), (), s32[]{:S(2)}) async-start(), calls=%async_computation.1 | async-start | bytes 19183616 | tf_op jit(solution)/shard_map/all_gather | solution.py:91
  13.2 621.2 %all-reduce.2.cloned.1.call-start = ((), (), s32[]{:S(2)}) async-start(), calls=%async_computation | async-start | bytes 131072 | tf_op jit(solution)/shard_map/psum | solution.py:21
  298.4 132.5 %copy-start.17 = (s32[2]{0:T(128)S(1)}, s32[2]{0:T(128)}, u32[]{:S(2)}) copy-start(s32[2]{0:T(128)} %param.29) | copy-start | bytes 28
  298.4 133.1 %copy-start.9 = (f32[2,2,2432]{2,1,0:T(2,128)S(1)}, f32[2,2,2432]{2,1,0:T(2,128)}, u32[]{:S(2)}) copy-start(f32[2,2,2432]{2,1,0:T(2,128)} %param.26) | copy-start | bytes 116740
  348.5 13.1 %copy-start.3 = (f32[2,256,1216]{1,2,0:T(8,128)S(1)}, f32[2,256,1216]{1,2,0:T(8,128)}, u32[]{:S(2)}) copy-start(f32[2,256,1216]{1,2,0:T(8,128)} %get-tuple-element.177) | copy-start | bytes 7471108 | tf_op jit(solution)/shard_map/cond
  363.5 52.4 %copy-start.10 = (f32[2,2432]{1,0:T(2,128)S(1)}, f32[2,2432]{1,0:T(2,128)}, u32[]{:S(2)}) copy-start(f32[2,2432]{1,0:T(2,128)} %get-tuple-element.181) | copy-start | bytes 58372 | tf_op jit(solution)/shard_map/cond
  367.1 1.3 copy-start.5
  393.1 1.3 copy-start.5
  428.0 1.5 copy-start.1
  429.4 55.1 %collective-permute-start = (bf16[2,256,2432]{2,1,0:T(8,128)(2,1)}, bf16[2,256,2432]{2,1,0:T(8,128)(2,1)S(1)}, u32[]{:S(2)}, u32[]{:S(2)}) collective-permute-start(bf16[2,256,2432]{2,1,0:T(8,128)(2,1)} %copy-done.1), channel_id=1, source_target_pairs={{0,64},{1,65},{2,66},{3,67},{4,68},{5,69},{6,70},{7,71},{8,72},{9,... | collective-permute-start | bytes 7471112 | tf_op jit(solution)/shard_map/ppermute | solution.py:16
  488.9 1.2 copy-start.12
  488.9 1.2 copy-start.13
  492.0 142.4 %copy-start.8 = (f32[2,128,64]{1,2,0:T(8,128)S(1)}, f32[2,128,64]{1,2,0:T(8,128)}, u32[]{:S(2)}) copy-start(f32[2,128,64]{1,2,0:T(8,128)} %param.28) | copy-start | bytes 196612
  492.0 142.4 %copy-start.15 = (f32[2]{0:T(128)S(1)}, f32[2]{0:T(128)}, u32[]{:S(2)}) copy-start(f32[2]{0:T(128)} %get-tuple-element.171) | copy-start | bytes 28
  492.0 142.4 %copy-start.16 = (f32[2]{0:T(128)S(1)}, f32[2]{0:T(128)}, u32[]{:S(2)}) copy-start(f32[2]{0:T(128)} %get-tuple-element.172) | copy-start | bytes 28
Sparse Core Ops, SparseCore 0:
  10.4 67.5 all-gather.10
  80.2 97.6 all-gather.8
  180.5 117.8 all-gather.6
  492.1 142.2 all-reduce.1
where the time goes:
time: 652 us; the launch traced here: 643 us
  waiting for transfers between devices  478 us (73%)
  matrix products  67.2 us (10%)
  local copies, waits for them, and re-layouts  40.7 us (6%)
  other arithmetic  37.8 us (6%)
  between operations  14.4 us (2%)
    psum x1, waiting for transfers between devices, spread(): return lax.psum(jnp.where(mine, array, jnp.zeros_like(array)), axis)  139 us
    all_gather x1, waiting for transfers between devices, on_device(): lax.all_gather(qkv_weight[0], 'shard', axis=0, tiled=True)  120 us
    all_gather x1, waiting for transfers between devices, on_device(): stale_all = lax.all_gather(stale_kv[0], 'patch', axis=1, tiled=True)  100 us
    all_gather x1, waiting for transfers between devices, on_device(): lax.all_gather(out_weight[0], 'shard', axis=1, tiled=True)  64.7 us
    ppermute x1, waiting for transfers between devices, passed_along(): lax.ppermute(value, axis, [(source, source + steps) for source in range(f...  52.4 us
    dot_general x2, matrix products, attend_one(): jnp.einsum('hqk,khe->qhe', weights, values, preferred_element_type=jnp.fl...  21.8 us
    dot_general x2, matrix products, attend_one(): jnp.einsum('qhe,khe->hqk', query, keys, preferred_element_type=jnp.float32)  19.4 us
    dot_general x1, matrix products, run_layer(): jnp.einsum('rid,dc->ric', normed, w_qkv, preferred_element_type=jnp.float32)  16.5 us
  transfers between devices with their start and end apart: 5, of which 5 were waited for; matrix products, arithmetic and copies ran while one was open for 1% of the time, Pallas kernels for 0%

commit v1 on v0

--- a/solution.py
+++ b/solution.py
@@ -88,7 +88,10 @@
     step_index,
 ):
     w_qkv, w_out = (
-        lax.all_gather(qkv_weight[0], "shard", axis=0, tiled=True),
+        jnp.concatenate(
+            lax.all_to_all(jnp.stack([qkv_weight[0]] * lax.axis_size("shard")), "shard", 0, 0),
+            axis=0,
+        ),
         lax.all_gather(out_weight[0], "shard", axis=1, tiled=True),
     )
     stale_all = lax.all_gather(stale_kv[0], "patch", axis=1, tiled=True)

time: 652 us -> 728 us (1.12)
  waiting for transfers between devices: 478 us -> 536 us
  starting transfers between devices: 1.59 us -> 10.7 us
  local copies, waits for them, and re-layouts: 40.7 us -> 48.2 us
    all_gather x1, waiting for transfers between devices: 64.7 us -> 225 us  [on_device(): lax.all_gather(out_weight[0], 'shard', axis=1, tiled=True)]
    all_gather x1 -> x0, waiting for transfers between devices: 120 us -> none  [on_device(): lax.all_gather(qkv_weight[0], 'shard', axis=0, tiled=True)]
    all_gather x1, waiting for transfers between devices: 100 us -> 117 us  [on_device(): stale_all = lax.all_gather(stale_kv[0], 'patch', axis=1, tiled=True)]
    all_to_all x0 -> x1, starting transfers between devices: none -> 9.13 us  [on_device(): lax.all_to_all(jnp.stack([qkv_weight[0]] * lax.axis_size('shard')), 'shar...]
  transfers between devices with their start and end apart: 5 -> 5, of which waited for: 5 -> 4; matrix products, arithmetic and copies ran while one was open for 1% -> 2% of each run, Pallas kernels for 0% -> 0%
where the time goes in v1:
time: 728 us; the launch traced here: 718 us
  waiting for transfers between devices  536 us (74%)
  matrix products  67.2 us (9%)
  local copies, waits for them, and re-layouts  48.2 us (7%)
  other arithmetic  37.8 us (5%)
  between operations  14.4 us (2%)
  starting transfers between devices  10.7 us (1%)
    all_gather x1, waiting for transfers between devices, on_device(): lax.all_gather(out_weight[0], 'shard', axis=1, tiled=True)  225 us
    psum x1, waiting for transfers between devices, spread(): return lax.psum(jnp.where(mine, array, jnp.zeros_like(array)), axis)  143 us
    all_gather x1, waiting for transfers between devices, on_device(): stale_all = lax.all_gather(stale_kv[0], 'patch', axis=1, tiled=True)  117 us
    ppermute x1, waiting for transfers between devices, passed_along(): lax.ppermute(value, axis, [(source, source + steps) for source in range(f...  50.9 us
    dot_general x2, matrix products, attend_one(): jnp.einsum('hqk,khe->qhe', weights, values, preferred_element_type=jnp.fl...  21.8 us
    dot_general x2, matrix products, attend_one(): jnp.einsum('qhe,khe->hqk', query, keys, preferred_element_type=jnp.float32)  19.4 us
    dot_general x1, matrix products, run_layer(): jnp.einsum('rid,dc->ric', normed, w_qkv, preferred_element_type=jnp.float32)  16.5 us
  transfers between devices with their start and end apart: 5, of which 4 were waited for; matrix products, arithmetic and copies ran while one was open for 2% of the time, Pallas kernels for 0%

profile of v1, /device:TPU:1, one launch (start us, length us, event | category | flops | bytes accessed | tf_op | source)
XLA Modules:
  0.0 717.6 jit_solution(16488259281013142612)
XLA Ops:
  8.5 7.0 stack.3
  15.4 9.1 %all-to-all-start = ((bf16[16,152,3648]{2,1,0:T(8,128)(2,1)}), bf16[16,152,3648]{2,1,0:T(8,128)(2,1)}, u32[]{:S(2)}, u32[]{:S(2)}) async-start(bf16[16,152,3648]{2,1,0:T(8,128)(2,1)} %stack.3), calls=%async_computation | async-start | bytes 36110336 | tf_op jit(solution)/shard_map/all_to_all | solution.py:92
  24.7 4.5 copy.29
  29.2 224.6 %all-gather.7.cloned.1.call-done = bf16[1,1216,2432]{1,2,0:T(8,128)(2,1)} async-done(((bf16[1,1216,152]{1,2,0:T(8,128)(2,1)}), bf16[1,1216,2432]{1,2,0:T(8,128)(2,1)}) %all-gather.7.cloned.1.call-update) | async-done | bytes 5914640 | tf_op jit(solution)/shard_map/all_gather | solution.py:95
  253.8 116.9 %all-gather.5.cloned.1.call-done = bf16[1,2,1024,2432]{2,3,1,0:T(8,128)(2,1)} async-done(((bf16[1,2,256,2432]{2,3,1,0:T(8,128)(2,1)}), bf16[1,2,1024,2432]{2,3,1,0:T(8,128)(2,1)}) %all-gather.5.cloned.1.call-update) | async-done | bytes 9961488 | tf_op jit(solution)/shard_map/all_gather | solution.py:97
  370.7 129.3 %conditional.2 = (bf16[2,256,2432]{2,1,0:T(8,128)(2,1)S(1)}, bf16[2,256,2432]{2,1,0:T(8,128)(2,1)}) conditional(s32[]{:T(128)} %convert_element_type.88, bf16[2,256,2432]{2,1,0:T(8,128)(2,1)S(1)} %copy-done.2, (bf16[2,256,2432]{2,1,0:T(8,128)(2,1)S(1)}, f32[1,2,3,2432]{3,1,2,0:T(2,128)S(1)}, bf16[2432,3648]{1,0:T(8,128)(2,1)}, f32[1,64]{1,0:T(1,128)S(1)}, ...), branch_computations={%region_0.0_spmd, %region_1.9_spmd} | conditional | flops 13646128128 | bytes 220811024 | solution.py:109
  372.6 16.5 %fusion.6 = f32[2,256,3648]{1,2,0:T(8,128)} fusion(bf16[2432,3648]{1,0:T(8,128)(2,1)} %get-tuple-element.139, bf16[2,256,2432]{2,1,0:T(8,128)(2,1)S(1)} %get-tuple-element.71, f32[2,2432]{1,0:T(2,128)S(1)} %get-tuple-element.182, f32[2,2432]{1,0:T(2,128)S(1)} %get-tuple-element.183, f32[2,256]{1,0:T(2,128)S(1)} %add_rsqrt_fusion.2, ...), kind=kOutput, calls=%fused_computation.11 | convolution fusion | flops 9092333568 | bytes 27748352 | tf_op jit(solution)/shard_map/cond/branch_1_fun/rid,dc->ric/dot_general | solution.py:55
  389.1 3.3 slice_multiply_fusion
  392.4 2.0 reduce_sum.99
  394.4 4.7 fusion.76
  399.0 2.9 slice.91
  401.9 8.8 %copy.63 = bf16[2,1024,2432]{1,2,0:T(8,128)(2,1)} copy(bf16[2,1024,2432]{1,2,0:T(8,128)(2,1)} %get-tuple-element.74) | data formatting | bytes 19922944 | tf_op jit(solution)/shard_map/cond
  410.7 4.3 pad_maximum_fusion.1
  415.0 5.8 copy.31
  420.8 13.1 %pad_maximum_fusion = bf16[2,1178,2432]{1,2,0:T(8,128)(2,1)} fusion(bf16[2,1024,2432]{1,2,0:T(8,128)(2,1)} %get-tuple-element.180, bf16[2,154,2432]{1,2,0:T(8,128)(2,1)} %bitcast.148), kind=kLoop, calls=%fused_computation.13 | loop fusion | flops 22919168 | bytes 22919168 | tf_op jit(solution)/shard_map/cond/branch_1_fun/concatenate | solution.py:66
  434.3 1.5 multiply_convert_fusion
  435.8 52.1 %while.18 = (s32[]{:T(128)}, bf16[2,256,1216]{1,2,0:T(8,128)(2,1)}, bf16[2,1178,2432]{1,2,0:T(8,128)(2,1)}, bf16[2,256,19,64]{1,3,2,0:T(8,128)(2,1)}, s32[]{:T(128)}) while((s32[]{:T(128)}, bf16[2,256,1216]{1,2,0:T(8,128)(2,1)}, bf16[2,1178,2432]{1,2,0:T(8,128)(2,1)}, bf16[2,256,19,64]{1,3,2,0:T(8,128)(2,1)}, s32[]{:T(128)}) %tuple.88), condition=%wide.region_8.8_spmd, body=%wide.region_6.7_spmd.sunk | while | flops 1478904064 | bytes 82245984 | solution.py:71
  435.9 3.2 dynamic-slice_bitcast_fusion.5
  440.4 9.7 %exponential_reduce_fusion.5 = (f32[19,256]{1,0:T(8,128)S(1)}, f32[19,256,1178]{1,2,0:T(8,128)}) fusion(bf16[1178,19,64]{0,2,1:T(8,128)(2,1)S(1)} %bitcast.135, bf16[2,256,19,64]{1,3,2,0:T(8,128)(2,1)S(1)} %copy-done.5, s32[]{:T(128)} %get-tuple-element.287), kind=kOutput, calls=%fused_computation.clone.1 | convolution fusion | flops 739138304 | bytes 26674180 | tf_op jit(solution)/shard_map/cond/branch_1_fun/while/body/eval_jaxpr/qhe,khe->hqk/dot_general | solution.py:40
  450.1 10.9 %divide_convert_fusion.5 = bf16[256,19,64]{0,2,1:T(8,128)(2,1)S(1)} fusion(bf16[1178,19,64]{0,2,1:T(8,128)(2,1)S(1)} %bitcast.137, f32[19,256,1178]{1,2,0:T(8,128)} %get-tuple-element.265, f32[256,19]{0,1:T(8,128)S(1)} %bitcast.151), kind=kOutput, calls=%fused_computation.5.clone.1 | convolution fusion | flops 739765760 | bytes 26426112 | tf_op jit(solution)/shard_map/cond/branch_1_fun/while/body/eval_jaxpr/hqk,khe->qhe/dot_general | solution.py:44
  461.9 3.2 dynamic-slice_bitcast_fusion.5
  466.3 9.7 %exponential_reduce_fusion.5 = (f32[19,256]{1,0:T(8,128)S(1)}, f32[19,256,1178]{1,2,0:T(8,128)}) fusion(bf16[1178,19,64]{0,2,1:T(8,128)(2,1)S(1)} %bitcast.135, bf16[2,256,19,64]{1,3,2,0:T(8,128)(2,1)S(1)} %copy-done.5, s32[]{:T(128)} %get-tuple-element.287), kind=kOutput, calls=%fused_computation.clone.1 | convolution fusion | flops 739138304 | bytes 26674180 | tf_op jit(solution)/shard_map/cond/branch_1_fun/while/body/eval_jaxpr/qhe,khe->hqk/dot_general | solution.py:40
  476.0 10.9 %divide_convert_fusion.5 = bf16[256,19,64]{0,2,1:T(8,128)(2,1)S(1)} fusion(bf16[1178,19,64]{0,2,1:T(8,128)(2,1)S(1)} %bitcast.137, f32[19,256,1178]{1,2,0:T(8,128)} %get-tuple-element.265, f32[256,19]{0,1:T(8,128)S(1)} %bitcast.151), kind=kOutput, calls=%fused_computation.5.clone.1 | convolution fusion | flops 739765760 | bytes 26426112 | tf_op jit(solution)/shard_map/cond/branch_1_fun/while/body/eval_jaxpr/hqk,khe->qhe/dot_general | solution.py:44
  487.8 7.6 %fusion.19 = bf16[2,256,2432]{2,1,0:T(8,128)(2,1)S(1)} fusion(bf16[2,256,2432]{2,1,0:T(8,128)(2,1)S(1)} %get-tuple-element.71, bf16[2,256,1216]{1,2,0:T(8,128)(2,1)} %get-tuple-element.78, bf16[1216,2432]{0,1:T(8,128)(2,1)} %get-tuple-element.144, f32[2,2432]{1,0:T(2,128)S(1)} %copy-done.11), kind=kOutput, calls=%fused_computation.26 | convolution fusion | flops 3033268224 | bytes 12160000 | tf_op jit(solution)/shard_map/cond/branch_1_fun/riw,wd->rid/dot_general | solution.py:72
  495.5 4.3 copy.47
  504.2 50.9 %collective-permute-done = bf16[2,256,2432]{2,1,0:T(8,128)(2,1)S(1)} collective-permute-done((bf16[2,256,2432]{2,1,0:T(8,128)(2,1)}, bf16[2,256,2432]{2,1,0:T(8,128)(2,1)S(1)}, u32[]{:S(2)}, u32[]{:S(2)}) %collective-permute-start) | collective-permute-done | bytes 2490400 | tf_op jit(solution)/shard_map/ppermute | solution.py:16
  555.1 4.4 conditional.3
  555.1 1.6 broadcast.162.clone
  560.7 1.8 fusion.69
  562.6 3.4 select_bitcast_fusion
  566.0 143.0 %all-reduce.2.cloned.1.call-done = bf16[2,256,64]{1,2,0:T(8,128)(2,1)} async-done(((bf16[2,256,64]{1,2,0:T(8,128)(2,1)}), bf16[2,256,64]{1,2,0:T(8,128)(2,1)}) %all-reduce.2.cloned.1.call-update) | async-done | bytes 65552 | tf_op jit(solution)/shard_map/psum | solution.py:21
  709.1 1.5 fusion.73
  (62 shorter events, 13.3 us)
Async XLA Ops:
  7.2 553.5 %copy-start = (bf16[2432,64]{0,1:T(8,128)(2,1)S(1)}, bf16[2432,64]{0,1:T(8,128)(2,1)}, u32[]{:S(2)}) copy-start(bf16[2432,64]{0,1:T(8,128)(2,1)} %param.27) | copy-start | bytes 933892
  7.2 1.3 copy-start.7
  7.2 246.6 %all-gather.7.cloned.1.call-start = ((), (), s32[]{:S(2)}) async-start(), calls=%async_computation.3 | async-start | bytes 6615040 | tf_op jit(solution)/shard_map/all_gather | solution.py:95
  15.4 355.2 %all-to-all-start = ((bf16[16,152,3648]{2,1,0:T(8,128)(2,1)}), bf16[16,152,3648]{2,1,0:T(8,128)(2,1)}, u32[]{:S(2)}, u32[]{:S(2)}) async-start(bf16[16,152,3648]{2,1,0:T(8,128)(2,1)} %stack.3), calls=%async_computation | async-start | bytes 36110336 | tf_op jit(solution)/shard_map/all_to_all | solution.py:92
  24.6 346.1 %copy-start.2 = (bf16[2,256,2432]{2,1,0:T(8,128)(2,1)S(1)}, bf16[2,256,2432]{2,1,0:T(8,128)(2,1)}, u32[]{:S(2)}) copy-start(bf16[2,256,2432]{2,1,0:T(8,128)(2,1)} %param.19) | copy-start | bytes 7471108
  24.6 346.1 %copy-start.8 = (f32[1,2,3,2432]{3,1,2,0:T(2,128)S(1)}, f32[1,2,3,2432]{3,1,2,0:T(2,128)}, u32[]{:S(2)}) copy-start(f32[1,2,3,2432]{3,1,2,0:T(2,128)} %param.22) | copy-start | bytes 175108
  24.6 346.1 %copy-start.15 = (f32[1,64]{1,0:T(1,128)S(1)}, f32[1,64]{1,0:T(1,128)}, u32[]{:S(2)}) copy-start(f32[1,64]{1,0:T(1,128)} %param.23) | copy-start | bytes 772
  24.6 346.1 %all-gather.5.cloned.1.call-start = ((), (), s32[]{:S(2)}) async-start(), calls=%async_computation.2 | async-start | bytes 12451840 | tf_op jit(solution)/shard_map/all_gather | solution.py:97
  29.2 679.9 %all-reduce.2.cloned.1.call-start = ((), (), s32[]{:S(2)}) async-start(), calls=%async_computation.1 | async-start | bytes 131072 | tf_op jit(solution)/shard_map/psum | solution.py:21
  370.7 132.2 %copy-start.18 = (s32[2]{0:T(128)S(1)}, s32[2]{0:T(128)}, u32[]{:S(2)}) copy-start(s32[2]{0:T(128)} %param.29) | copy-start | bytes 28
  370.7 132.8 %copy-start.10 = (f32[2,2,2432]{2,1,0:T(2,128)S(1)}, f32[2,2,2432]{2,1,0:T(2,128)}, u32[]{:S(2)}) copy-start(f32[2,2,2432]{2,1,0:T(2,128)} %param.26) | copy-start | bytes 116740
  420.8 13.1 %copy-start.3 = (f32[2,256,1216]{1,2,0:T(8,128)S(1)}, f32[2,256,1216]{1,2,0:T(8,128)}, u32[]{:S(2)}) copy-start(f32[2,256,1216]{1,2,0:T(8,128)} %get-tuple-element.177) | copy-start | bytes 7471108 | tf_op jit(solution)/shard_map/cond
  435.8 52.1 %copy-start.11 = (f32[2,2432]{1,0:T(2,128)S(1)}, f32[2,2432]{1,0:T(2,128)}, u32[]{:S(2)}) copy-start(f32[2,2432]{1,0:T(2,128)} %get-tuple-element.181) | copy-start | bytes 58372 | tf_op jit(solution)/shard_map/cond
  439.1 1.3 copy-start.5
  465.1 1.3 copy-start.5
  500.0 1.5 copy-start.1
  501.5 53.6 %collective-permute-start = (bf16[2,256,2432]{2,1,0:T(8,128)(2,1)}, bf16[2,256,2432]{2,1,0:T(8,128)(2,1)S(1)}, u32[]{:S(2)}, u32[]{:S(2)}) collective-permute-start(bf16[2,256,2432]{2,1,0:T(8,128)(2,1)} %copy-done.1), channel_id=1, source_target_pairs={{0,64},{1,65},{2,66},{3,67},{4,68},{5,69},{6,70},{7,71},{8,72},{9,... | collective-permute-start | bytes 7471112 | tf_op jit(solution)/shard_map/ppermute | solution.py:16
  559.5 1.2 copy-start.13
  559.5 1.2 copy-start.14
  562.6 146.5 %copy-start.9 = (f32[2,128,64]{1,2,0:T(8,128)S(1)}, f32[2,128,64]{1,2,0:T(8,128)}, u32[]{:S(2)}) copy-start(f32[2,128,64]{1,2,0:T(8,128)} %param.28) | copy-start | bytes 196612
  562.6 146.5 %copy-start.16 = (f32[2]{0:T(128)S(1)}, f32[2]{0:T(128)}, u32[]{:S(2)}) copy-start(f32[2]{0:T(128)} %get-tuple-element.171) | copy-start | bytes 28
  562.6 146.5 %copy-start.17 = (f32[2]{0:T(128)S(1)}, f32[2]{0:T(128)}, u32[]{:S(2)}) copy-start(f32[2]{0:T(128)} %get-tuple-element.172) | copy-start | bytes 28
Sparse Core Ops, SparseCore 0:
  10.4 243.3 all-gather.6
  256.0 114.5 all-gather.4
  562.7 146.3 all-reduce.1
